TPU v7x, 32 devices: a whole 2x2x4 slice. The times are simulated.
32 devices in a mesh: dp: 8 (over y, x, core), fsdp: 4 (over z).
Axes of the slice: x: 2, y: 2, z: 4, core: 2. Of those that a mesh axis runs over, the one named last changes fastest.
Arguments:
- inputs: bfloat16 [32, 512, 1024], P(('dp', 'fsdp')), may hold values from -6 to 6
- segment_ids: int32 [32, 512], P(('dp', 'fsdp')), may hold values from 0 to 6, as said below
- query_weight: bfloat16 [1024, 1024], P(('dp', 'fsdp')), may hold values from -0.1875 to 0.1875
- key_weight: bfloat16 [1024, 1024], P(('dp', 'fsdp')), may hold values from -0.1875 to 0.1875
- value_weight: bfloat16 [1024, 1024], P(('dp', 'fsdp')), may hold values from -0.1875 to 0.1875
- output_weight: bfloat16 [1024, 1024], P(('dp', 'fsdp')), may hold values from -1 to 1
- query_bias: bfloat16 [1024], P(('dp', 'fsdp')), may hold values from -3 to 3
- value_bias: bfloat16 [1024], P(('dp', 'fsdp')), may hold values from -3 to 3
- output_bias: bfloat16 [1024], P(('dp', 'fsdp')), may hold values from -3 to 3
- attn_gain: bfloat16 [1024], P(('dp', 'fsdp')), may hold values from 0.5 to 1.5
- attn_shift: bfloat16 [1024], P(('dp', 'fsdp')), may hold values from -2 to 2
- inner_weight: bfloat16 [1024, 4096], P(('dp', 'fsdp')), may hold values from -0.1875 to 0.1875
- inner_bias: bfloat16 [4096], P(('dp', 'fsdp')), may hold values from -3 to 3
- outer_weight: bfloat16 [4096, 1024], P(('dp', 'fsdp')), may hold values from -0.125 to 0.125
- outer_bias: bfloat16 [1024], P(('dp', 'fsdp')), may hold values from -3 to 3
- ffn_gain: bfloat16 [1024], P(('dp', 'fsdp')), may hold values from 0.5 to 1.5
- ffn_shift: bfloat16 [1024], P(('dp', 'fsdp')), may hold values from -2 to 2
- out_grad: bfloat16 [32, 512, 1024], P(('dp', 'fsdp')), may hold values from -6 to 6
Outputs:
- outputs: bfloat16 [32, 512, 1024], P(('dp', 'fsdp'))
- input_grad: float32 [32, 512, 1024], P(('dp', 'fsdp'))
- grad_query_weight: float32 [1024, 1024], P(('dp', 'fsdp'))
- grad_key_weight: float32 [1024, 1024], P(('dp', 'fsdp'))
- grad_value_weight: float32 [1024, 1024], P(('dp', 'fsdp'))
- grad_output_weight: float32 [1024, 1024], P(('dp', 'fsdp'))
- grad_query_bias: float32 [1024], P(('dp', 'fsdp'))
- grad_value_bias: float32 [1024], P(('dp', 'fsdp'))
- grad_output_bias: float32 [1024], P(('dp', 'fsdp'))
- grad_attn_gain: float32 [1024], P(('dp', 'fsdp'))
- grad_attn_shift: float32 [1024], P(('dp', 'fsdp'))
- grad_inner_weight: float32 [1024, 4096], P(('dp', 'fsdp'))
- grad_inner_bias: float32 [4096], P(('dp', 'fsdp'))
- grad_outer_weight: float32 [4096, 1024], P(('dp', 'fsdp'))
- grad_outer_bias: float32 [1024], P(('dp', 'fsdp'))
- grad_ffn_gain: float32 [1024], P(('dp', 'fsdp'))
- grad_ffn_shift: float32 [1024], P(('dp', 'fsdp'))
Inputs may be any that keep to these rules, and one draw needn't show every extreme that they name: `segment_ids`: in each row the document numbers start at 1, never fall and rise by one at each new document, up to 6 documents; padding (0) is a tail of at most 128 positions.
All inputs are finite; a program needn't handle non-finite values.
Results may differ from a plain program's by a relative error of at most 0.014.
Values may be sent and summed in bfloat16 or wider, within the bound.
No kernel may reach another device: no remote copies, remote signals or barrier semaphores. Data moves between devices by JAX's collectives and lax.ppermute only.
A program may use at most 256 MiB of HBM per device.

v0:
```python
import jax
import jax.numpy as jnp
from jax import lax
from jax.sharding import PartitionSpec as P

H = 16
HD = 64
EPSILON = 1e-05


def scaled_norm(rows_in, gain):
    row_mean = jnp.mean(rows_in, axis=-1, keepdims=True)
    centred = rows_in - row_mean
    spread = jnp.mean(centred * centred, axis=-1, keepdims=True)
    return centred * lax.rsqrt(spread + EPSILON) * gain


def gelu_exact(value_in):
    return jax.nn.gelu(value_in, approximate=False)


def to_groups(matrix, row_count, seq_len):
    groups = H // 4
    shaped = matrix.reshape(row_count, seq_len, groups, 4, HD).transpose(0, 2, 1, 3, 4)
    return shaped.reshape(row_count * groups, seq_len, 4, HD)


def from_groups(stacked, row_count, seq_len):
    groups = stacked.shape[0] // row_count
    shaped = stacked.reshape(row_count, groups, seq_len, 4, HD).transpose(0, 2, 1, 3, 4)
    return shaped.reshape(row_count * seq_len, groups * 4 * HD)


def masked_scores(query_block, key_block, seg_row):
    score_scale = HD ** (-0.5)
    scores = (
        jnp.einsum("qhd,khd->hqk", query_block, key_block, preferred_element_type=jnp.float32)
        * score_scale
    )
    same_doc = seg_row[:, None] == seg_row[None, :]
    return jnp.where(same_doc[None], scores, -1e30)


def attend_forward(item_set):
    query_block, key_block, value_block, seg_row = item_set
    scores = masked_scores(query_block, key_block, seg_row)
    row_max = jnp.max(scores, axis=-1, keepdims=True)
    raised = jnp.exp(scores - row_max)
    row_total = jnp.sum(raised, axis=-1, keepdims=True)
    prob_low = (raised / row_total).astype(jnp.bfloat16)
    mixed_block = jnp.einsum(
        "hqk,khd->qhd", prob_low, value_block, preferred_element_type=jnp.float32
    )
    return (mixed_block, (row_max + jnp.log(row_total))[..., 0])


def attend_backward(item_set):
    query_block, key_block, value_block, seg_row, mixed_grad, log_total = item_set
    score_scale = HD ** (-0.5)
    scores = masked_scores(query_block, key_block, seg_row)
    probabilities = jnp.exp(scores - log_total[..., None])
    prob_low = probabilities.astype(jnp.bfloat16)
    value_grad = jnp.einsum(
        "hqk,qhd->khd", prob_low, mixed_grad, preferred_element_type=jnp.float32
    )
    prob_grad = jnp.einsum(
        "qhd,khd->hqk", mixed_grad, value_block, preferred_element_type=jnp.float32
    )
    inner_sum = jnp.sum(probabilities * prob_grad, axis=-1, keepdims=True)
    score_grad = (probabilities * (prob_grad - inner_sum)).astype(jnp.bfloat16)
    query_grad = (
        jnp.einsum("hqk,khd->qhd", score_grad, key_block, preferred_element_type=jnp.float32)
        * score_scale
    )
    key_grad = (
        jnp.einsum("hqk,qhd->khd", score_grad, query_block, preferred_element_type=jnp.float32)
        * score_scale
    )
    return (query_grad, key_grad, value_grad)


def matmul(left, right):
    return jnp.dot(left, right, preferred_element_type=jnp.float32)


def column_sum(matrix):
    return jnp.sum(matrix.astype(jnp.float32), axis=0)


def shards(
    inputs,
    segment_ids,
    query_weight,
    key_weight,
    value_weight,
    output_weight,
    query_bias,
    value_bias,
    output_bias,
    attn_gain,
    attn_shift,
    inner_weight,
    inner_bias,
    outer_weight,
    outer_bias,
    ffn_gain,
    ffn_shift,
    out_grad,
):
    row_count, seq_len, model_width = inputs.shape
    tokens_here = row_count * seq_len
    flattened = inputs.reshape(tokens_here, model_width)
    (
        query_full,
        key_full,
        value_full,
        output_full,
        query_bias_full,
        value_bias_full,
        output_bias_full,
        attn_gain_full,
        attn_shift_full,
    ) = (
        lax.all_gather(query_weight, ("dp", "fsdp"), axis=0, tiled=True),
        lax.all_gather(key_weight, ("dp", "fsdp"), axis=0, tiled=True),
        lax.all_gather(value_weight, ("dp", "fsdp"), axis=0, tiled=True),
        lax.all_gather(output_weight, ("dp", "fsdp"), axis=0, tiled=True),
        lax.all_gather(query_bias, ("dp", "fsdp"), axis=0, tiled=True),
        lax.all_gather(value_bias, ("dp", "fsdp"), axis=0, tiled=True),
        lax.all_gather(output_bias, ("dp", "fsdp"), axis=0, tiled=True),
        lax.all_gather(attn_gain, ("dp", "fsdp"), axis=0, tiled=True),
        lax.all_gather(attn_shift, ("dp", "fsdp"), axis=0, tiled=True),
    )
    queries = (matmul(flattened, query_full) + query_bias_full.astype(jnp.float32)).astype(
        jnp.bfloat16
    )
    key_rows = matmul(flattened, key_full).astype(jnp.bfloat16)
    value_rows = (matmul(flattened, value_full) + value_bias_full.astype(jnp.float32)).astype(
        jnp.bfloat16
    )
    query_groups = to_groups(queries, row_count, seq_len)
    key_groups = to_groups(key_rows, row_count, seq_len)
    value_groups = to_groups(value_rows, row_count, seq_len)
    seg_repeat = jnp.repeat(segment_ids, H // 4, axis=0)
    group_mixed, log_totals = lax.map(
        attend_forward, (query_groups, key_groups, value_groups, seg_repeat)
    )
    mixed_low = from_groups(group_mixed, row_count, seq_len).astype(jnp.bfloat16)
    attn_branch = matmul(mixed_low, output_full) + output_bias_full.astype(jnp.float32)
    attn_sum = flattened.astype(jnp.float32) + attn_branch
    attn_normed = scaled_norm(
        attn_sum, attn_gain_full.astype(jnp.float32)
    ) + attn_shift_full.astype(jnp.float32)
    normed_low = attn_normed.astype(jnp.bfloat16)
    inner_full, inner_bias_full, outer_full, outer_bias_full, ffn_gain_full, ffn_shift_full = (
        lax.all_gather(inner_weight, ("dp", "fsdp"), axis=0, tiled=True),
        lax.all_gather(inner_bias, ("dp", "fsdp"), axis=0, tiled=True),
        lax.all_gather(outer_weight, ("dp", "fsdp"), axis=0, tiled=True),
        lax.all_gather(outer_bias, ("dp", "fsdp"), axis=0, tiled=True),
        lax.all_gather(ffn_gain, ("dp", "fsdp"), axis=0, tiled=True),
        lax.all_gather(ffn_shift, ("dp", "fsdp"), axis=0, tiled=True),
    )
    inner_pre = matmul(normed_low, inner_full) + inner_bias_full.astype(jnp.float32)
    act_low = gelu_exact(inner_pre).astype(jnp.bfloat16)
    ffn_branch = matmul(act_low, outer_full) + outer_bias_full.astype(jnp.float32)
    ffn_sum = attn_normed + ffn_branch
    outputs = (
        scaled_norm(ffn_sum, ffn_gain_full.astype(jnp.float32)) + ffn_shift_full.astype(jnp.float32)
    ).astype(jnp.bfloat16)
    inner_back, outer_back, ffn_gain_back = (
        lax.all_gather(inner_weight, ("dp", "fsdp"), axis=0, tiled=True),
        lax.all_gather(outer_weight, ("dp", "fsdp"), axis=0, tiled=True),
        lax.all_gather(ffn_gain, ("dp", "fsdp"), axis=0, tiled=True),
    )
    grad_out = out_grad.reshape(tokens_here, model_width).astype(jnp.float32)
    _, ffn_norm_pull = jax.vjp(scaled_norm, ffn_sum, ffn_gain_back.astype(jnp.float32))
    grad_ffn_sum, grad_ffn_gain = ffn_norm_pull(grad_out)
    grad_ffn_shift = jnp.sum(grad_out, axis=0)
    branch_grad = grad_ffn_sum.astype(jnp.bfloat16)
    grad_outer_bias = column_sum(branch_grad)
    grad_outer = jnp.einsum("nf,nd->fd", act_low, branch_grad, preferred_element_type=jnp.float32)
    grad_act = jnp.einsum("nd,fd->nf", branch_grad, outer_back, preferred_element_type=jnp.float32)
    _, gelu_pull = jax.vjp(gelu_exact, inner_pre)
    inner_grad = gelu_pull(grad_act)[0].astype(jnp.bfloat16)
    grad_inner_bias = column_sum(inner_grad)
    grad_inner = jnp.einsum("nd,nf->df", normed_low, inner_grad, preferred_element_type=jnp.float32)
    grad_normed = grad_ffn_sum + jnp.einsum(
        "nf,df->nd", inner_grad, inner_back, preferred_element_type=jnp.float32
    )
    ffn_terms = (
        grad_inner,
        grad_inner_bias,
        grad_outer,
        grad_outer_bias,
        grad_ffn_gain,
        grad_ffn_shift,
    )
    ffn_owned = (
        lax.psum_scatter(ffn_terms[0], ("dp", "fsdp"), scatter_dimension=0, tiled=True),
        lax.psum_scatter(ffn_terms[1], ("dp", "fsdp"), scatter_dimension=0, tiled=True),
        lax.psum_scatter(ffn_terms[2], ("dp", "fsdp"), scatter_dimension=0, tiled=True),
        lax.psum_scatter(ffn_terms[3], ("dp", "fsdp"), scatter_dimension=0, tiled=True),
        lax.psum_scatter(ffn_terms[4], ("dp", "fsdp"), scatter_dimension=0, tiled=True),
        lax.psum_scatter(ffn_terms[5], ("dp", "fsdp"), scatter_dimension=0, tiled=True),
    )
    (
        shard_inner,
        shard_inner_bias,
        shard_outer,
        shard_outer_bias,
        shard_ffn_gain,
        shard_ffn_shift,
    ) = ffn_owned
    query_back, key_back, value_back, output_back, attn_gain_back = (
        lax.all_gather(query_weight, ("dp", "fsdp"), axis=0, tiled=True),
        lax.all_gather(key_weight, ("dp", "fsdp"), axis=0, tiled=True),
        lax.all_gather(value_weight, ("dp", "fsdp"), axis=0, tiled=True),
        lax.all_gather(output_weight, ("dp", "fsdp"), axis=0, tiled=True),
        lax.all_gather(attn_gain, ("dp", "fsdp"), axis=0, tiled=True),
    )
    _, attn_norm_pull = jax.vjp(scaled_norm, attn_sum, attn_gain_back.astype(jnp.float32))
    grad_attn_sum, grad_attn_gain = attn_norm_pull(grad_normed)
    grad_attn_shift = jnp.sum(grad_normed, axis=0)
    attn_grad = grad_attn_sum.astype(jnp.bfloat16)
    grad_output_bias = column_sum(attn_grad)
    grad_output = jnp.einsum("nd,ne->de", mixed_low, attn_grad, preferred_element_type=jnp.float32)
    mixed_grad = jnp.einsum(
        "ne,de->nd", attn_grad, output_back, preferred_element_type=jnp.float32
    ).astype(jnp.bfloat16)
    group_qgrad, group_kgrad, group_vgrad = lax.map(
        attend_backward,
        (
            query_groups,
            key_groups,
            value_groups,
            seg_repeat,
            to_groups(mixed_grad, row_count, seq_len),
            log_totals,
        ),
    )
    query_grad = from_groups(group_qgrad, row_count, seq_len).astype(jnp.bfloat16)
    key_grad = from_groups(group_kgrad, row_count, seq_len).astype(jnp.bfloat16)
    value_grad = from_groups(group_vgrad, row_count, seq_len).astype(jnp.bfloat16)
    grad_query_bias = column_sum(query_grad)
    grad_value_bias = column_sum(value_grad)
    grad_query = jnp.einsum("nd,ne->de", flattened, query_grad, preferred_element_type=jnp.float32)
    grad_key = jnp.einsum("nd,ne->de", flattened, key_grad, preferred_element_type=jnp.float32)
    grad_value = jnp.einsum("nd,ne->de", flattened, value_grad, preferred_element_type=jnp.float32)
    input_grad = (
        grad_attn_sum
        + jnp.einsum("ne,de->nd", query_grad, query_back, preferred_element_type=jnp.float32)
        + jnp.einsum("ne,de->nd", key_grad, key_back, preferred_element_type=jnp.float32)
        + jnp.einsum("ne,de->nd", value_grad, value_back, preferred_element_type=jnp.float32)
    )
    attn_owned = (
        lax.psum_scatter(grad_query, ("dp", "fsdp"), scatter_dimension=0, tiled=True),
        lax.psum_scatter(grad_key, ("dp", "fsdp"), scatter_dimension=0, tiled=True),
        lax.psum_scatter(grad_value, ("dp", "fsdp"), scatter_dimension=0, tiled=True),
        lax.psum_scatter(grad_output, ("dp", "fsdp"), scatter_dimension=0, tiled=True),
        lax.psum_scatter(grad_query_bias, ("dp", "fsdp"), scatter_dimension=0, tiled=True),
        lax.psum_scatter(grad_value_bias, ("dp", "fsdp"), scatter_dimension=0, tiled=True),
        lax.psum_scatter(grad_output_bias, ("dp", "fsdp"), scatter_dimension=0, tiled=True),
        lax.psum_scatter(grad_attn_gain, ("dp", "fsdp"), scatter_dimension=0, tiled=True),
        lax.psum_scatter(grad_attn_shift, ("dp", "fsdp"), scatter_dimension=0, tiled=True),
    )
    (
        shard_query,
        shard_key,
        shard_value,
        shard_output,
        shard_query_bias,
        shard_value_bias,
        shard_output_bias,
        shard_attn_gain,
        shard_attn_shift,
    ) = attn_owned
    return (
        outputs.reshape(row_count, seq_len, model_width),
        input_grad.reshape(row_count, seq_len, model_width),
        shard_query,
        shard_key,
        shard_value,
        shard_output,
        shard_query_bias,
        shard_value_bias,
        shard_output_bias,
        shard_attn_gain,
        shard_attn_shift,
        shard_inner,
        shard_inner_bias,
        shard_outer,
        shard_outer_bias,
        shard_ffn_gain,
        shard_ffn_shift,
    )


def solution(mesh):
    placed = (
        P(("dp", "fsdp"), None, None),
        P(("dp", "fsdp"), None),
        P(("dp", "fsdp"), None),
        P(("dp", "fsdp"), None),
        P(("dp", "fsdp"), None),
        P(("dp", "fsdp"), None),
        P(("dp", "fsdp")),
        P(("dp", "fsdp")),
        P(("dp", "fsdp")),
        P(("dp", "fsdp")),
        P(("dp", "fsdp")),
        P(("dp", "fsdp"), None),
        P(("dp", "fsdp")),
        P(("dp", "fsdp"), None),
        P(("dp", "fsdp")),
        P(("dp", "fsdp")),
        P(("dp", "fsdp")),
        P(("dp", "fsdp"), None, None),
    )
    return jax.shard_map(
        shards,
        mesh=mesh,
        in_specs=placed,
        out_specs=(
            P(("dp", "fsdp"), None, None),
            P(("dp", "fsdp"), None, None),
            P(("dp", "fsdp"), None),
            P(("dp", "fsdp"), None),
            P(("dp", "fsdp"), None),
            P(("dp", "fsdp"), None),
            P(("dp", "fsdp")),
            P(("dp", "fsdp")),
            P(("dp", "fsdp")),
            P(("dp", "fsdp")),
            P(("dp", "fsdp")),
            P(("dp", "fsdp"), None),
            P(("dp", "fsdp")),
            P(("dp", "fsdp"), None),
            P(("dp", "fsdp")),
            P(("dp", "fsdp")),
            P(("dp", "fsdp")),
        ),
        check_vma=False,
    )
```

profile of v0, /device:TPU:0, one launch (start us, length us, event | category | flops | bytes accessed | tf_op | source)
XLA Modules:
  0.0 1826.1 jit_solution(2462448369746053519)
XLA Ops:
  17.9 42.3 %all-reduce.18 = (bf16[1024]{0:T(1024)(128)(2,1)S(1)}, bf16[1024]{0:T(1024)(128)(2,1)S(1)}, bf16[1024]{0:T(1024)(128)(2,1)S(1)}, bf16[1024]{0:T(1024)(128)(2,1)S...) all-reduce(bf16[1024]{0:T(1024)(128)(2,1)S(1)} %dynamic-update-slic, ...), channel_id=1, replica_groups=mesh['dp'=8,'fsdp'=4] {'dp','fsdp'}, use_global_device_ids=true, to_apply=%add | all-reduce | flops 8192 | bytes 32768
  60.3 65.7 %all-gather = bf16[32,1,128]{2,1,0:T(2,128)(2,1)S(1)} all-gather(bf16[1,1,128]{2,1,0:T(2,128)(2,1)} %bitcast.239), channel_id=1, replica_groups=mesh['dp'=8,'fsdp'=4] {'dp','fsdp'}, dimensions={0}, use_global_device_ids=true | all-gather | bytes 8448 | tf_op jit(solution)/shard_map/all_gather | solution.py:157
  126.0 3.2 add_convert_fusion.3
  129.8 3.2 add_convert_fusion.2
  133.6 53.3 %all-gather.12.cloned.1.call-done = bf16[1024,1024]{1,0:T(8,128)(2,1)} async-done(((bf16[32,1024]{1,0:T(8,128)(2,1)}), bf16[1024,1024]{1,0:T(8,128)(2,1)}) %all-gather.12.cloned.1.call-update) | async-done | bytes 2097168 | tf_op jit(solution)/shard_map/all_gather | solution.py:125
  186.9 4.1 convolution_convert_fusion.1
  191.1 1.5 copy.63
  193.7 16.7 while.26
  195.8 2.1 fusion.137
  199.9 2.1 fusion.137
  204.1 2.1 fusion.137
  208.2 2.1 fusion.137
  210.3 34.8 %all-gather.14.cloned.1.call-done = bf16[1024,1024]{1,0:T(8,128)(2,1)} async-done(((bf16[32,1024]{1,0:T(8,128)(2,1)}), bf16[1024,1024]{1,0:T(8,128)(2,1)}) %all-gather.14.cloned.1.call-update) | async-done | bytes 2097168 | tf_op jit(solution)/shard_map/all_gather | solution.py:127
  245.1 3.5 fusion.82
  248.7 1.3 copy-done
  250.3 73.9 %all-gather.16.cloned.1.call-done = bf16[1024,4096]{1,0:T(8,128)(2,1)} async-done(((bf16[32,4096]{1,0:T(8,128)(2,1)}), bf16[1024,4096]{1,0:T(8,128)(2,1)}) %all-gather.16.cloned.1.call-update) | async-done | bytes 8388624 | tf_op jit(solution)/shard_map/all_gather | solution.py:156
  324.2 28.1 %multiply_convert_fusion.1 = (bf16[512,4096]{1,0:T(8,128)(2,1)}, f32[512,4096]{1,0:T(8,128)}, f32[512,4096]{1,0:T(8,128)}) fusion(f32[4096]{0:T(1024)S(1)} %bitcast.236, bf16[1024,4096]{1,0:T(8,128)(2,1)} %all-gather.16.cloned.1.call-done, f32[512,1024]{1,0:T(8,128)} %copy-done, f32[1024]{0:T(1024)S(1)} %convert_element_type.165, ...), kind=kOutput, calls=%fused_computation.66 | convolution fusion | flops 4436000768 | bytes 31485952 | tf_op jit(solution)/shard_map/dot_general | solution.py:83
  352.3 50.7 %all-gather.18.cloned.1.call-done = bf16[4096,1024]{1,0:T(8,128)(2,1)} async-done(((bf16[128,1024]{1,0:T(8,128)(2,1)}), bf16[4096,1024]{1,0:T(8,128)(2,1)}) %all-gather.18.cloned.1.call-update) | async-done | bytes 8388624 | tf_op jit(solution)/shard_map/all_gather | solution.py:158
  403.0 10.0 fusion.83
  414.2 1.9 fusion.80
  416.4 15.4 convert_reduce_fusion
  431.8 8.9 multiply_reduce_fusion.1
  441.4 1.3 copy-done.3
  443.9 1.3 convolution_convert_fusion
  445.2 1.4 copy.64
  446.5 1.1 broadcast.230
  447.6 1.1 broadcast.230.clone.1
  448.8 34.5 %while.27 = (s32[]{:T(128)}, bf16[4,512,4,64]{1,3,2,0:T(8,128)(2,1)}, bf16[4,512,4,64]{1,3,2,0:T(8,128)(2,1)}, bf16[4,512,4,64]{1,3,2,0:T(8,128)(2,1)S(1)}, bf16...) while((s32[]{:T(128)}, ...), condition=%wide.region_14.15_spmd, body=%wide.region_12.14_spmd.sunk | while | flops 687339520 | bytes 56954112 | solution.py:230
  450.5 2.5 multiply_reduce_fusion.6
  453.0 1.3 multiply_convert_fusion.3
  456.5 1.2 fusion.149
  459.0 2.5 multiply_reduce_fusion.6
  461.5 1.3 multiply_convert_fusion.3
  465.1 1.2 fusion.149
  467.5 2.5 multiply_reduce_fusion.6
  470.0 1.3 multiply_convert_fusion.3
  473.6 1.2 fusion.149
  476.1 2.5 multiply_reduce_fusion.6
  478.5 1.3 multiply_convert_fusion.3
  482.1 1.2 fusion.149
  483.4 4.7 convolution_bitcast_fusion.2
  488.1 5.3 copy.72
  493.5 1.1 copy-done.20
  494.9 3.2 convolution_bitcast_fusion.1
  498.1 5.4 copy.74
  503.6 3.2 convolution_bitcast_fusion
  506.7 5.4 copy.76
  512.3 1.1 copy-done.17
  513.4 4.4 fusion.86
  517.9 1.5 copy-done.2
  519.4 10.6 fusion.75
  530.1 1.1 copy-done.15
  531.3 10.4 fusion.87
  541.7 1.2 copy-done.6
  543.8 40.5 %all-reduce.17 = (f32[1024]{0:T(1024)S(1)}, f32[1024]{0:T(1024)S(1)}, f32[1024]{0:T(1024)S(1)}, f32[1024]{0:T(1024)S(1)}, f32[1024]{0:T(1024)S(1)}, /*index=5*/f...) all-reduce(f32[1024]{0:T(1024)S(1)} %reduce_sum.191, ...), channel_id=6, replica_groups=mesh['dp'=8,'fsdp'=4] {'dp','fsdp'}, use_global_device_ids=true, to_apply=%region_20.21.clone | all-reduce | flops 12288 | bytes 98304
  589.6 3.0 fusion.84
  592.6 1.3 fusion.85
  594.9 2.9 add_bitcast_fusion
  597.7 42.6 %reduce-scatter.19.cloned.1.call-done = f32[32,1024]{1,0:T(8,128)} async-done(((f32[1024,1024]{1,0:T(8,128)}), f32[32,1024]{1,0:T(8,128)}) %reduce-scatter.19.cloned.1.call-update) | async-done | bytes 131088
  640.3 149.2 %reduce-scatter.21.cloned.1.call-done = f32[32,1024]{1,0:T(8,128)} async-done(((f32[1024,1024]{1,0:T(8,128)}), f32[32,1024]{1,0:T(8,128)}) %reduce-scatter.21.cloned.1.call-update) | async-done | bytes 131088
  789.6 149.7 %reduce-scatter.23.cloned.1.call-done = f32[32,1024]{1,0:T(8,128)} async-done(((f32[1024,1024]{1,0:T(8,128)}), f32[32,1024]{1,0:T(8,128)}) %reduce-scatter.23.cloned.1.call-update) | async-done | bytes 131088
  939.3 149.4 %reduce-scatter.13.cloned.1.call-done = f32[32,1024]{1,0:T(8,128)} async-done(((f32[1024,1024]{1,0:T(8,128)}), f32[32,1024]{1,0:T(8,128)}) %reduce-scatter.13.cloned.1.call-update) | async-done | bytes 131088 | tf_op jit(solution)/shard_map/reduce_scatter | solution.py:259
  1088.7 365.5 %reduce-scatter.15.cloned.1.call-done = f32[32,4096]{1,0:T(8,128)} async-done(((f32[1024,4096]{1,0:T(8,128)}), f32[32,4096]{1,0:T(8,128)}) %reduce-scatter.15.cloned.1.call-update) | async-done | bytes 524304 | tf_op jit(solution)/shard_map/reduce_scatter | solution.py:199
  1454.2 364.9 %reduce-scatter.17.cloned.1.call-done = f32[128,1024]{1,0:T(8,128)} async-done(((f32[4096,1024]{1,0:T(8,128)}), f32[128,1024]{1,0:T(8,128)}) %reduce-scatter.17.cloned.1.call-update) | async-done | bytes 524304 | tf_op jit(solution)/shard_map/reduce_scatter | solution.py:201
  (201 shorter events, 46.3 us)
Async XLA Ops:
  7.2 118.9 %all-gather.8.cloned.1.call-start = ((), (), s32[]{:S(2)}) async-start(), calls=%async_computation.6 | async-start | bytes 2162688 | tf_op jit(solution)/shard_map/all_gather | solution.py:126
  7.9 121.9 %all-gather.10.cloned.1.call-start = ((), (), s32[]{:S(2)}) async-start(), calls=%async_computation.7 | async-start | bytes 2162688 | tf_op jit(solution)/shard_map/all_gather | solution.py:124
  8.7 178.3 %all-gather.12.cloned.1.call-start = ((), (), s32[]{:S(2)}) async-start(), calls=%async_computation.8 | async-start | bytes 2162688 | tf_op jit(solution)/shard_map/all_gather | solution.py:125
  9.4 235.7 %all-gather.14.cloned.1.call-start = ((), (), s32[]{:S(2)}) async-start(), calls=%async_computation.9 | async-start | bytes 2162688 | tf_op jit(solution)/shard_map/all_gather | solution.py:127
  10.0 314.2 %all-gather.16.cloned.1.call-start = ((), (), s32[]{:S(2)}) async-start(), calls=%async_computation.10 | async-start | bytes 8650752 | tf_op jit(solution)/shard_map/all_gather | solution.py:156
  10.6 392.4 %all-gather.18.cloned.1.call-start = ((), (), s32[]{:S(2)}) async-start(), calls=%async_computation.11 | async-start | bytes 8650752 | tf_op jit(solution)/shard_map/all_gather | solution.py:158
  11.1 629.2 %reduce-scatter.19.cloned.1.call-start = ((), (), s32[]{:S(2)}) async-start(), calls=%async_computation.15 | async-start | bytes 4325376
  133.6 59.0 %copy-start.23 = (s32[1,512]{1,0:T(1,128)S(1)}, s32[1,512]{1,0:T(1,128)}, u32[]{:S(2)}) copy-start(s32[1,512]{1,0:T(1,128)} %param.23) | copy-start | bytes 6148
  210.3 40.0 %copy-start.7 = (bf16[4,512,4,64]{1,3,2,0:T(8,128)(2,1)}, bf16[4,512,4,64]{1,3,2,0:T(8,128)(2,1)S(1)}, u32[]{:S(2)}) copy-start(bf16[4,512,4,64]{1,3,2,0:T(8,128)(2,1)S(1)} %get-tuple-element.439) | copy-start | bytes 3145732
  248.7 1.3 copy-start
  403.0 10.4 copy-start.5
  416.3 15.4 copy-start.14
  416.3 15.4 copy-start.1
  440.7 3.2 copy-start.12
  441.3 1.3 copy-start.3
  442.9 1.0 copy-start.16
  449.3 1.2 copy-start.8
  453.0 1.3 copy-start.18
  453.0 2.1 copy-start.9
  455.0 1.5 copy-start.19
  455.5 1.0 copy-start.10
  457.8 1.2 copy-start.8
  461.5 1.3 copy-start.18
  461.5 2.1 copy-start.9
  463.5 1.5 copy-start.19
  464.0 1.0 copy-start.10
  466.3 1.2 copy-start.8
  470.0 1.3 copy-start.18
  470.0 2.1 copy-start.9
  472.1 1.5 copy-start.19
  472.6 1.0 copy-start.10
  474.8 1.2 copy-start.8
  478.5 1.3 copy-start.18
  478.5 2.1 copy-start.9
  480.6 1.5 copy-start.19
  481.1 1.0 copy-start.10
  493.4 1.2 copy-start.20
  493.4 1.5 copy-start.22
  493.4 296.1 %reduce-scatter.21.cloned.1.call-start = ((), (), s32[]{:S(2)}) async-start(), calls=%async_computation.16 | async-start | bytes 4325376
  503.5 435.8 %reduce-scatter.23.cloned.1.call-start = ((), (), s32[]{:S(2)}) async-start(), calls=%async_computation.17 | async-start | bytes 4325376
  512.2 1.2 copy-start.17
  512.2 576.5 %reduce-scatter.13.cloned.1.call-start = ((), (), s32[]{:S(2)}) async-start(), calls=%async_computation.12 | async-start | bytes 4325376 | tf_op jit(solution)/shard_map/reduce_scatter | solution.py:259
  517.8 1.6 copy-start.2
  517.9 936.3 %reduce-scatter.15.cloned.1.call-start = ((), (), s32[]{:S(2)}) async-start(), calls=%async_computation.13 | async-start | bytes 17301504 | tf_op jit(solution)/shard_map/reduce_scatter | solution.py:199
  530.1 1.2 copy-start.15
  530.1 1289.0 %reduce-scatter.17.cloned.1.call-start = ((), (), s32[]{:S(2)}) async-start(), calls=%async_computation.14 | async-start | bytes 17301504 | tf_op jit(solution)/shard_map/reduce_scatter | solution.py:201
  541.7 1.2 copy-start.6
  541.7 1.6 copy-start.11
  589.6 3.1 copy-start.21
  589.6 3.1 copy-start.24
  592.6 1.6 copy-start.4
  592.6 2.2 copy-start.13
Sparse Core Ops, SparseCore 0:
  10.9 59.3 all-gather.7
  73.2 55.3 all-gather.9
  131.6 55.3 all-gather.11
  189.7 55.3 all-gather.13
  247.9 76.2 all-gather.15
  327.0 75.9 all-gather.17
  493.6 146.7 reduce-scatter.18
  643.2 146.3 reduce-scatter.20
  792.4 146.8 reduce-scatter.22
  942.0 146.7 reduce-scatter.12
  1091.6 362.5 reduce-scatter.14
  1456.9 362.1 reduce-scatter.16
where the time goes:
time: 1840 us; the launch traced here: 1830 us
  waiting for transfers between devices  1440 us (78%)
  matrix products  156 us (8%)
  blocking collectives  149 us (8%)
  local copies, waits for them, and re-layouts  51.7 us (3%)
    reduce_scatter x1, waiting for transfers between devices, shards(): lax.psum_scatter(ffn_terms[0], ('dp', 'fsdp'), scatter_dimension=0, tiled...  365 us
    reduce_scatter x1, waiting for transfers between devices, shards(): lax.psum_scatter(ffn_terms[2], ('dp', 'fsdp'), scatter_dimension=0, tiled...  365 us
    unnamed x15, waiting for transfers between devices  345 us
    reduce_scatter x1, waiting for transfers between devices, shards(): lax.psum_scatter(grad_output, ('dp', 'fsdp'), scatter_dimension=0, tiled=...  149 us
    unnamed x2, blocking collectives  82.8 us
    all_gather x1, waiting for transfers between devices, shards(): lax.all_gather(inner_weight, ('dp', 'fsdp'), axis=0, tiled=True)  73.9 us
    all_gather x1, blocking collectives, shards(): lax.all_gather(inner_bias, ('dp', 'fsdp'), axis=0, tiled=True)  65.7 us
    all_gather x1, waiting for transfers between devices, shards(): lax.all_gather(key_weight, ('dp', 'fsdp'), axis=0, tiled=True)  53.3 us
  transfers between devices with their start and end apart: 12, of which 10 were waited for; matrix products, arithmetic and copies ran while one was open for 7% of the time, Pallas kernels for 0%

commit v1 on v0

--- a/solution.py
+++ b/solution.py
@@ -110,6 +110,19 @@
     row_count, seq_len, model_width = inputs.shape
     tokens_here = row_count * seq_len
     flattened = inputs.reshape(tokens_here, model_width)
+
+    def _write_block(values):
+        axis_name = ("dp", "fsdp")
+        earlier, odd = (lax.axis_size(axis_name), lax.axis_index(axis_name))
+        w2, moved = (values, 1)
+        while moved < earlier:
+            state_next = lax.ppermute(w2, axis_name, [(dev, dev ^ moved) for dev in range(earlier)])
+            seen_now = jnp.concatenate([w2, state_next], axis=0)
+            h_now = jnp.concatenate([state_next, w2], axis=0)
+            w2 = jnp.where(odd & moved == 0, seen_now, h_now)
+            moved = 2 * moved
+        return w2
+
     (
         query_full,
         key_full,
@@ -122,7 +135,7 @@
         attn_shift_full,
     ) = (
         lax.all_gather(query_weight, ("dp", "fsdp"), axis=0, tiled=True),
-        lax.all_gather(key_weight, ("dp", "fsdp"), axis=0, tiled=True),
+        _write_block(key_weight),
         lax.all_gather(value_weight, ("dp", "fsdp"), axis=0, tiled=True),
         lax.all_gather(output_weight, ("dp", "fsdp"), axis=0, tiled=True),
         lax.all_gather(query_bias, ("dp", "fsdp"), axis=0, tiled=True),

time: 1840 us -> 1750 us (0.951)
  waiting for transfers between devices: 1440 us -> 1310 us
  matrix products: 156 us -> 175 us
    reduce_scatter x1, waiting for transfers between devices: 149 us -> 0.01 us  [shards(): lax.psum_scatter(grad_output, ('dp', 'fsdp'), scatter_dimension=0, tiled=...]
    unnamed x15, waiting for transfers between devices: 345 us -> 448 us
    all_gather x1, waiting for transfers between devices: 53.3 us -> 0.01 us  [shards(): lax.all_gather(key_weight, ('dp', 'fsdp'), axis=0, tiled=True)]
    all_gather x1, waiting for transfers between devices: 34.8 us -> 0.01 us  [shards(): lax.all_gather(output_weight, ('dp', 'fsdp'), axis=0, tiled=True)]
    ppermute x0 -> x5, waiting for transfers between devices: none -> 22.5 us  [_write_block(): lax.ppermute(w2, axis_name, [(dev, dev ^ moved) for dev in range(earlier)])]
    unnamed x68 -> x78, local copies, waits for them, and re-layouts: 39.2 us -> 30.6 us
  transfers between devices with their start and end apart: 12 -> 17, of which waited for: 10 -> 11; matrix products, arithmetic and copies ran while one was open for 7% -> 13% of each run, Pallas kernels for 0% -> 0%
where the time goes in v1:
time: 1750 us; the launch traced here: 1740 us
  waiting for transfers between devices  1310 us (75%)
  matrix products  175 us (10%)
  blocking collectives  165 us (9%)
  local copies, waits for them, and re-layouts  43.9 us (3%)
  other arithmetic  18.6 us (1%)
    unnamed x15, waiting for transfers between devices  448 us
    reduce_scatter x1, waiting for transfers between devices, shards(): lax.psum_scatter(ffn_terms[0], ('dp', 'fsdp'), scatter_dimension=0, tiled...  365 us
    reduce_scatter x1, waiting for transfers between devices, shards(): lax.psum_scatter(ffn_terms[2], ('dp', 'fsdp'), scatter_dimension=0, tiled...  365 us
    unnamed x2, blocking collectives  101 us
    all_gather x1, blocking collectives, shards(): lax.all_gather(inner_bias, ('dp', 'fsdp'), axis=0, tiled=True)  64.9 us
    all_gather x1, waiting for transfers between devices, shards(): lax.all_gather(inner_weight, ('dp', 'fsdp'), axis=0, tiled=True)  61.7 us
    all_gather x1, waiting for transfers between devices, shards(): lax.all_gather(outer_weight, ('dp', 'fsdp'), axis=0, tiled=True)  51.3 us
    dot_general x6, matrix products, matmul(): return jnp.dot(left, right, preferred_element_type=jnp.float32)  48.5 us
  transfers between devices with their start and end apart: 17, of which 11 were waited for; matrix products, arithmetic and copies ran while one was open for 13% of the time, Pallas kernels for 0%

profile of v1, /device:TPU:0, one launch (start us, length us, event | category | flops | bytes accessed | tf_op | source)
XLA Modules:
  0.0 1741.9 jit_solution(13887695356112175459)
XLA Ops:
  10.7 3.1 collective-permute-start
  13.8 2.5 collective-permute-done
  17.2 3.1 collective-permute-start.1
  20.3 5.2 collective-permute-done.1
  25.6 1.5 collective-permute-done.2
  27.3 1.6 collective-permute-start.3
  28.9 13.3 collective-permute-done.3
  42.7 1.6 collective-permute-start.4
  46.3 59.7 %all-reduce.18 = (bf16[1024]{0:T(1024)(128)(2,1)S(1)}, bf16[1024]{0:T(1024)(128)(2,1)S(1)}, bf16[1024]{0:T(1024)(128)(2,1)S(1)}, bf16[1024]{0:T(1024)(128)(2,1)S...) all-reduce(bf16[1024]{0:T(1024)(128)(2,1)S(1)} %dynamic-update-slic, ...), channel_id=1, replica_groups=mesh['dp'=8,'fsdp'=4] {'dp','fsdp'}, use_global_device_ids=true, to_apply=%add | all-reduce | flops 8192 | bytes 32768
  106.1 64.9 %all-gather = bf16[32,1,128]{2,1,0:T(2,128)(2,1)S(1)} all-gather(bf16[1,1,128]{2,1,0:T(2,128)(2,1)S(1)} %bitcast.238), channel_id=1, replica_groups=mesh['dp'=8,'fsdp'=4] {'dp','fsdp'}, dimensions={0}, use_global_device_ids=true | all-gather | bytes 8448 | tf_op jit(solution)/shard_map/all_gather | solution.py:170
  171.0 2.9 fusion.73
  174.0 2.8 add_convert_fusion.3
  178.3 2.9 add_convert_fusion.2
  182.8 20.6 %while.26 = (s32[]{:T(128)}, bf16[4,512,4,64]{1,3,2,0:T(8,128)(2,1)}, f32[4,4,512]{2,1,0:T(4,128)S(1)}, bf16[4,512,4,64]{1,3,2,0:T(8,128)(2,1)}, s32[4,512]{1,0:...) while((s32[]{:T(128)}, ...), condition=%wide.region_3.4_spmd, body=%wide.region_0.3_spmd.sunk | while | flops 281278464 | bytes 15016029 | solution.py:158
  184.9 3.1 fusion.145
  190.1 3.0 fusion.145
  195.2 3.0 fusion.145
  200.3 3.1 fusion.145
  204.4 3.5 fusion.91
  208.3 61.7 %all-gather.14.cloned.1.call-done = bf16[1024,4096]{1,0:T(8,128)(2,1)} async-done(((bf16[32,4096]{1,0:T(8,128)(2,1)}), bf16[1024,4096]{1,0:T(8,128)(2,1)}) %all-gather.14.cloned.1.call-update) | async-done | bytes 8388624 | tf_op jit(solution)/shard_map/all_gather | solution.py:169
  270.1 27.7 %multiply_convert_fusion.1 = (bf16[512,4096]{1,0:T(8,128)(2,1)}, f32[512,4096]{1,0:T(8,128)}, f32[512,4096]{1,0:T(8,128)}) fusion(f32[4096]{0:T(1024)S(1)} %bitcast.235, bf16[1024,4096]{1,0:T(8,128)(2,1)} %all-gather.14.cloned.1.call-done, f32[512,1024]{1,0:T(8,128)S(1)} %get-tuple-element.239, f32[1024]{0:T(1024)S(1)} %convert_element_type.169, ...), kind=kOutput, calls=%fused_computation.66 | convolution fusion | flops 4436000768 | bytes 31485952 | tf_op jit(solution)/shard_map/dot_general | solution.py:83
  297.7 51.3 %all-gather.16.cloned.1.call-done = bf16[4096,1024]{1,0:T(8,128)(2,1)} async-done(((bf16[128,1024]{1,0:T(8,128)(2,1)}), bf16[4096,1024]{1,0:T(8,128)(2,1)}) %all-gather.16.cloned.1.call-update) | async-done | bytes 8388624 | tf_op jit(solution)/shard_map/all_gather | solution.py:171
  349.0 8.7 fusion.92
  359.0 1.9 fusion.89
  361.1 13.8 convert_reduce_fusion
  374.9 9.1 multiply_reduce_fusion.1
  387.3 2.3 convolution_convert_fusion
  389.6 2.7 copy.61
  392.3 4.7 fusion.95
  400.4 44.7 %while.27 = (s32[]{:T(128)}, bf16[4,512,4,64]{1,3,2,0:T(8,128)(2,1)}, bf16[4,512,4,64]{1,3,2,0:T(8,128)(2,1)}, bf16[4,512,4,64]{1,3,2,0:T(8,128)(2,1)}, bf16[4,5...) while((s32[]{:T(128)}, ...), condition=%wide.region_14.15_spmd, body=%wide.region_12.14_spmd.sunk | while | flops 687339520 | bytes 56954112 | solution.py:243
  400.4 1.8 fusion.154
  402.5 2.5 multiply_reduce_fusion.6
  407.0 1.6 fusion.155
  409.6 1.9 fusion.157
  411.6 1.8 fusion.154
  413.6 2.5 multiply_reduce_fusion.6
  418.2 1.6 fusion.155
  420.8 2.0 fusion.157
  422.8 1.8 fusion.154
  424.8 2.5 multiply_reduce_fusion.6
  429.4 1.6 fusion.155
  432.0 2.0 fusion.157
  434.0 1.8 fusion.154
  436.0 2.5 multiply_reduce_fusion.6
  440.6 1.6 fusion.155
  443.2 2.0 fusion.157
  445.2 4.8 convolution_bitcast_fusion.2
  449.9 5.4 copy.69
  456.5 4.4 convolution_bitcast_fusion.1
  461.0 5.3 copy.71
  466.4 4.8 convolution_bitcast_fusion
  471.2 5.4 copy.73
  476.6 10.7 fusion.84
  488.5 10.4 fusion.96
  500.5 1.6 convert_reduce_fusion.4
  502.3 40.9 %all-reduce.17 = (f32[1024]{0:T(1024)S(1)}, f32[1024]{0:T(1024)S(1)}, f32[1024]{0:T(1024)S(1)}, f32[1024]{0:T(1024)S(1)}, f32[1024]{0:T(1024)S(1)}, /*index=5*/f...) all-reduce(f32[1024]{0:T(1024)S(1)} %reduce_sum.191, ...), channel_id=6, replica_groups=mesh['dp'=8,'fsdp'=4] {'dp','fsdp'}, use_global_device_ids=true, to_apply=%region_20.21.clone | all-reduce | flops 12288 | bytes 98304
  548.4 4.2 fusion.93
  552.6 3.0 fusion.94
  556.1 4.1 add_bitcast_fusion
  560.2 146.0 %reduce-scatter.19.cloned.1.call-done = f32[32,1024]{1,0:T(8,128)} async-done(((f32[1024,1024]{1,0:T(8,128)}), f32[32,1024]{1,0:T(8,128)}) %reduce-scatter.19.cloned.1.call-update) | async-done | bytes 131088
  706.2 149.5 %reduce-scatter.21.cloned.1.call-done = f32[32,1024]{1,0:T(8,128)} async-done(((f32[1024,1024]{1,0:T(8,128)}), f32[32,1024]{1,0:T(8,128)}) %reduce-scatter.21.cloned.1.call-update) | async-done | bytes 131088
  855.7 149.1 %reduce-scatter.23.cloned.1.call-done = f32[32,1024]{1,0:T(8,128)} async-done(((f32[1024,1024]{1,0:T(8,128)}), f32[32,1024]{1,0:T(8,128)}) %reduce-scatter.23.cloned.1.call-update) | async-done | bytes 131088
  1004.8 365.2 %reduce-scatter.15.cloned.1.call-done = f32[32,4096]{1,0:T(8,128)} async-done(((f32[1024,4096]{1,0:T(8,128)}), f32[32,4096]{1,0:T(8,128)}) %reduce-scatter.15.cloned.1.call-update) | async-done | bytes 524304 | tf_op jit(solution)/shard_map/reduce_scatter | solution.py:212
  1370.0 364.9 %reduce-scatter.17.cloned.1.call-done = f32[128,1024]{1,0:T(8,128)} async-done(((f32[4096,1024]{1,0:T(8,128)}), f32[128,1024]{1,0:T(8,128)}) %reduce-scatter.17.cloned.1.call-update) | async-done | bytes 524304 | tf_op jit(solution)/shard_map/reduce_scatter | solution.py:214
  (224 shorter events, 50.8 us)
Async XLA Ops:
  7.2 37.2 %copy-start.21 = (bf16[32]{0:T(256)(128)(2,1)S(1)}, bf16[32]{0:T(256)(128)(2,1)}, u32[]{:S(2)}) copy-start(bf16[32]{0:T(256)(128)(2,1)} %param.29) | copy-start | bytes 196
  7.2 37.5 %copy-start.22 = (bf16[32]{0:T(256)(128)(2,1)S(1)}, bf16[32]{0:T(256)(128)(2,1)}, u32[]{:S(2)}) copy-start(bf16[32]{0:T(256)(128)(2,1)} %param.28) | copy-start | bytes 196
  7.2 37.7 %copy-start.23 = (bf16[32]{0:T(256)(128)(2,1)S(1)}, bf16[32]{0:T(256)(128)(2,1)}, u32[]{:S(2)}) copy-start(bf16[32]{0:T(256)(128)(2,1)} %param.30) | copy-start | bytes 196
  7.2 37.9 %copy-start.24 = (bf16[32]{0:T(256)(128)(2,1)S(1)}, bf16[32]{0:T(256)(128)(2,1)}, u32[]{:S(2)}) copy-start(bf16[32]{0:T(256)(128)(2,1)} %param.31) | copy-start | bytes 196
  7.2 38.2 %copy-start.25 = (bf16[32]{0:T(256)(128)(2,1)S(1)}, bf16[32]{0:T(256)(128)(2,1)}, u32[]{:S(2)}) copy-start(bf16[32]{0:T(256)(128)(2,1)} %param.32) | copy-start | bytes 196
  7.2 38.4 %copy-start.26 = (bf16[32]{0:T(256)(128)(2,1)S(1)}, bf16[32]{0:T(256)(128)(2,1)}, u32[]{:S(2)}) copy-start(bf16[32]{0:T(256)(128)(2,1)} %param.36) | copy-start | bytes 196
  7.2 38.6 %copy-start.27 = (bf16[32]{0:T(256)(128)(2,1)S(1)}, bf16[32]{0:T(256)(128)(2,1)}, u32[]{:S(2)}) copy-start(bf16[32]{0:T(256)(128)(2,1)} %param.37) | copy-start | bytes 196
  7.3 38.8 %copy-start.28 = (bf16[32]{0:T(256)(128)(2,1)S(1)}, bf16[32]{0:T(256)(128)(2,1)}, u32[]{:S(2)}) copy-start(bf16[32]{0:T(256)(128)(2,1)} %param.38) | copy-start | bytes 196
  7.3 98.8 %copy-start.20 = (bf16[128]{0:T(256)(128)(2,1)S(1)}, bf16[128]{0:T(256)(128)(2,1)}, u32[]{:S(2)}) copy-start(bf16[128]{0:T(256)(128)(2,1)} %param.34) | copy-start | bytes 772
  7.3 163.8 %copy-start.18 = (bf16[1,512,1024]{2,1,0:T(8,128)(2,1)S(1)}, bf16[1,512,1024]{2,1,0:T(8,128)(2,1)}, u32[]{:S(2)}) copy-start(bf16[1,512,1024]{2,1,0:T(8,128)(2,1)} %param.22) | copy-start | bytes 3145732
  7.3 166.7 %all-gather.8.cloned.1.call-start = ((), (), s32[]{:S(2)}) async-start(), calls=%async_computation.6 | async-start | bytes 2162688 | tf_op jit(solution)/shard_map/all_gather | solution.py:139
  8.0 170.3 %all-gather.10.cloned.1.call-start = ((), (), s32[]{:S(2)}) async-start(), calls=%async_computation.7 | async-start | bytes 2162688 | tf_op jit(solution)/shard_map/all_gather | solution.py:137
  8.8 194.6 %all-gather.12.cloned.1.call-start = ((), (), s32[]{:S(2)}) async-start(), calls=%async_computation.8 | async-start | bytes 2162688 | tf_op jit(solution)/shard_map/all_gather | solution.py:140
  9.5 260.6 %all-gather.14.cloned.1.call-start = ((), (), s32[]{:S(2)}) async-start(), calls=%async_computation.9 | async-start | bytes 8650752 | tf_op jit(solution)/shard_map/all_gather | solution.py:169
  10.1 339.0 %all-gather.16.cloned.1.call-start = ((), (), s32[]{:S(2)}) async-start(), calls=%async_computation.10 | async-start | bytes 8650752 | tf_op jit(solution)/shard_map/all_gather | solution.py:171
  10.7 541.9 %all-gather.18.cloned.1.call-start = ((), (), s32[]{:S(2)}) async-start(), calls=%async_computation.11 | async-start | bytes 2162688 | tf_op jit(solution)/shard_map/all_gather | solution.py:229
  10.7 5.5 collective-permute-start
  17.2 8.3 collective-permute-start.1
  25.6 1.6 collective-permute-start.2
  27.3 14.9 collective-permute-start.3
  42.7 128.3 %collective-permute-start.4 = (bf16[512,1024]{1,0:T(8,128)(2,1)S(1)}, bf16[512,1024]{1,0:T(8,128)(2,1)}, u32[]{:S(2)}, u32[]{:S(2)}) collective-permute-start(bf16[512,1024]{1,0:T(8,128)(2,1)S(1)} %maximum_select_fusion.4), channel_id=1, source_target_pairs={{0,16},{1,17},{2,18},{3,19},{4,20},{5,21},{6,22},{7,23},{8,24},{9,... | collective-permute-start | bytes 3145736 | tf_op jit(solution)/shard_map/ppermute | solution.py:119
  44.3 515.9 %reduce-scatter.13.cloned.1.call-start = ((), (), s32[]{:S(2)}) async-start(), calls=%async_computation.12 | async-start | bytes 4325376 | tf_op jit(solution)/shard_map/reduce_scatter | solution.py:272
  178.3 3.4 copy-start.19
  203.4 1.0 copy-start.2
  349.0 9.1 copy-start.3
  361.1 13.8 copy-start.12
  374.9 9.1 copy-start.29
  384.1 3.2 copy-start.9
  384.8 1.3 copy-start
  386.4 1.0 copy-start.17
  397.0 309.2 %reduce-scatter.19.cloned.1.call-start = ((), (), s32[]{:S(2)}) async-start(), calls=%async_computation.15 | async-start | bytes 4325376
  400.4 2.1 copy-start.5
  404.9 1.3 copy-start.14
  405.0 2.1 copy-start.6
  407.0 2.6 copy-start.15
  408.7 1.0 copy-start.7
  411.6 2.1 copy-start.5
  416.1 1.3 copy-start.14
  416.1 2.1 copy-start.6
  418.2 2.6 copy-start.15
  419.8 1.0 copy-start.7
  422.8 2.1 copy-start.5
  427.3 1.3 copy-start.14
  427.3 2.1 copy-start.6
  429.4 2.6 copy-start.15
  431.0 1.0 copy-start.7
  434.0 2.1 copy-start.5
  438.5 1.3 copy-start.14
  438.5 2.1 copy-start.6
  440.6 2.6 copy-start.15
  442.2 1.0 copy-start.7
  455.3 1.2 copy-start.16
  455.3 400.4 %reduce-scatter.21.cloned.1.call-start = ((), (), s32[]{:S(2)}) async-start(), calls=%async_computation.16 | async-start | bytes 4325376
  466.3 538.5 %reduce-scatter.23.cloned.1.call-start = ((), (), s32[]{:S(2)}) async-start(), calls=%async_computation.17 | async-start | bytes 4325376
  476.6 893.4 %reduce-scatter.15.cloned.1.call-start = ((), (), s32[]{:S(2)}) async-start(), calls=%async_computation.13 | async-start | bytes 17301504 | tf_op jit(solution)/shard_map/reduce_scatter | solution.py:212
  487.3 1.2 copy-start.13
  487.3 1247.6 %reduce-scatter.17.cloned.1.call-start = ((), (), s32[]{:S(2)}) async-start(), calls=%async_computation.14 | async-start | bytes 17301504 | tf_op jit(solution)/shard_map/reduce_scatter | solution.py:214
  499.0 1.2 copy-start.4
  499.0 1.5 copy-start.8
  552.6 3.1 copy-start.1
  552.6 3.1 copy-start.10
  552.6 3.5 copy-start.11
Sparse Core Ops, SparseCore 0:
  11.1 63.1 all-gather.7
  77.1 55.4 all-gather.9
  135.6 55.3 all-gather.11
  193.8 76.2 all-gather.13
  272.8 76.1 all-gather.15
  351.8 55.0 all-gather.17
  409.8 146.8 reduce-scatter.12
  559.6 146.6 reduce-scatter.18
  709.1 146.5 reduce-scatter.20
  858.4 146.3 reduce-scatter.22
  1007.7 362.2 reduce-scatter.14
  1372.7 362.1 reduce-scatter.16
